TPU v7x, 32 devices: a whole 2x2x4 slice. The times are simulated.
32 devices in a mesh: groups: 2 (over y), trace: 4 (over z), space: 2 (over x), sub: 2 (over core).
Axes of the slice: x: 2, y: 2, z: 4, core: 2. Of those that a mesh axis runs over, the one named last changes fastest.
Arguments:
- seismic: bfloat16 [256, 1024, 128], P(('groups', 'trace', 'space', 'sub')), parts along dimension 0, may hold values from -6 to 6
- band_low: int32 [256], P('groups'), parts along dimension 0, may hold values from 0 to 127
- band_high: int32 [256], P('groups'), parts along dimension 0, may hold values from 256 to 512
- leaf_weights: bfloat16 [8, 512, 2, 64], replicated, may hold values from -0.15625 to 0.15625
- translations: float32 [32, 2, 64, 64], replicated, may hold values from -1 to 1
- level_table: int32 [3, 8, 2], replicated, may hold values from 0 to 31
Outputs:
- image_weights: float32 [16, 2, 64, 128], P(('groups', 'trace', 'space'), None, 'sub'), parts along dimension 0
There are 2 independent parts, one for each index of `groups`. A program takes and returns all parts, laid end to end along the dimension named above; an argument that names none is the same for every part. Nothing has to cross between parts.
All inputs are finite; a program needn't handle non-finite values.
Results may differ from a plain program's by a relative error of at most 0.0037.
Values may be sent and summed in bfloat16 or wider, within the bound.
No kernel may reach another device: no remote copies, remote signals or barrier semaphores. Data moves between devices by JAX's collectives and lax.ppermute only.
A program may use at most 64 MiB of HBM per device.

v0:
```python
import math

import jax
import jax.numpy as jnp
from jax import lax
from jax.sharding import PartitionSpec as P


def swapped(x, axis, distance):
    return lax.ppermute(x, axis, [(i, i ^ 1 << distance) for i in range(lax.axis_size(axis))])


def spectral_table(freq_total, samples):
    freq_range = jnp.arange(freq_total, dtype=jnp.int32)
    time_range = jnp.arange(samples, dtype=jnp.int32)
    phase = freq_range[:, None] * time_range[None, :] % samples
    angle = phase.astype(jnp.float32) * (2.0 * math.pi / samples)
    factor = 1.0 / math.sqrt(samples)
    return (jnp.concatenate([jnp.cos(angle), -jnp.sin(angle)], axis=0) * factor).astype(
        jnp.bfloat16
    )


def complex_product(left, right):
    highest = lax.Precision.HIGHEST
    real_part = jnp.dot(left[0], right[0], precision=highest) - jnp.dot(
        left[1], right[1], precision=highest
    )
    imag_part = jnp.dot(left[0], right[1], precision=highest) + jnp.dot(
        left[1], right[0], precision=highest
    )
    return jnp.stack([real_part, imag_part])


def swap_space(weights_now, bit_no):
    return swapped(weights_now, "space", bit_no)


def swap_trace(weights_now, bit_no):
    return swapped(weights_now, "trace", bit_no)


def merge_level(
    weights_now, partner, section_no, box_index, translations, level_table, sub_place, half_rank
):
    stride = 2**section_no
    upper_flag = box_index // stride % 2 == 1
    lower_part = jnp.where(upper_flag, partner, weights_now)
    upper_part = jnp.where(upper_flag, weights_now, partner)
    entries = lax.dynamic_index_in_dim(level_table[section_no], box_index, 0, keepdims=False)
    first_mat = lax.dynamic_index_in_dim(translations, entries[0], 0, keepdims=False)
    second_mat = lax.dynamic_index_in_dim(translations, entries[1], 0, keepdims=False)
    full_lower, full_upper = (
        lax.all_gather(lower_part, "sub", axis=1, tiled=True),
        lax.all_gather(upper_part, "sub", axis=1, tiled=True),
    )
    first_rows = lax.dynamic_slice_in_dim(first_mat, sub_place * half_rank, half_rank, 1)
    second_rows = lax.dynamic_slice_in_dim(second_mat, sub_place * half_rank, half_rank, 1)
    return complex_product(first_rows, full_lower) + complex_product(second_rows, full_upper)


def join_complex(parts):
    return jnp.stack([parts[:, 0, 0] - parts[:, 1, 1], parts[:, 0, 1] + parts[:, 1, 0]], axis=1)


def per_device(seismic, band_low, band_high, leaf_weights, translations, level_table):
    highest = lax.Precision.HIGHEST
    trace_count = lax.axis_size("trace")
    space_count = lax.axis_size("space")
    sub_count = lax.axis_size("sub")
    trace_place = lax.axis_index("trace")
    space_place = lax.axis_index("space")
    sub_place = lax.axis_index("sub")
    traces_here = seismic.shape[0]
    samples = seismic.shape[1]
    shots_count = seismic.shape[2]
    freq_total = leaf_weights.shape[1]
    rank_total = leaf_weights.shape[3]
    freq_block = freq_total // trace_count
    half_rank = rank_total // sub_count
    dft_rows = spectral_table(freq_total, samples)
    spectra = jnp.einsum(
        "kt,xts->xks", dft_rows, seismic, preferred_element_type=jnp.float32
    ).astype(jnp.bfloat16)
    spectra = spectra.reshape(traces_here, 2, freq_total, shots_count)
    freq_index = jnp.arange(freq_total, dtype=jnp.int32)
    band_mask = (
        (freq_index[:, None] >= band_low[None, :]) & (freq_index[:, None] < band_high[None, :])
    ).astype(jnp.bfloat16)
    masked = spectra * band_mask
    piece = masked.astype(jnp.float32)
    piece = piece.reshape(traces_here, 2, 1 * lax.axis_size("trace"), freq_block, shots_count)
    leaf_piece = leaf_weights.astype(jnp.float32)
    leaf_piece = leaf_piece.reshape(
        traces_here, 1 * lax.axis_size("trace"), freq_block, 2, rank_total
    )
    parts = jnp.einsum("iagfs,igfbr->gabrs", piece, leaf_piece, precision=highest)
    leaf_terms = lax.psum_scatter(join_complex(parts), "trace", scatter_dimension=0, tiled=True)[0]
    weights_now = lax.psum_scatter(leaf_terms, "sub", scatter_dimension=1, tiled=True)
    box_index = trace_place * space_count + space_place
    section_no = 0
    for bit_no in range(space_count.bit_length() - 1):
        partner = swap_space(weights_now, bit_no)
        weights_now = merge_level(
            weights_now,
            partner,
            section_no,
            box_index,
            translations,
            level_table,
            sub_place,
            half_rank,
        )
        section_no = section_no + 1
    for bit_no in range(trace_count.bit_length() - 1):
        partner = swap_trace(weights_now, bit_no)
        weights_now = merge_level(
            weights_now,
            partner,
            section_no,
            box_index,
            translations,
            level_table,
            sub_place,
            half_rank,
        )
        section_no = section_no + 1
    return weights_now[None]


def solution(mesh):
    placed = (
        P(("groups", "trace", "space", "sub"), None, None),
        P("groups"),
        P("groups"),
        P(),
        P(),
        P(),
    )
    return jax.shard_map(
        per_device,
        mesh=mesh,
        in_specs=placed,
        out_specs=P(("groups", "trace", "space"), None, "sub", None),
        check_vma=False,
    )
```

profile of v0, /device:TPU:0, one launch (start us, length us, event | category | flops | bytes accessed | tf_op | source)
XLA Modules:
  0.0 130.5 jit_solution(6518825922546346239)
XLA Ops:
  6.5 9.2 %sine_negate_fusion = (f32[512,1024]{1,0:T(8,128)}, f32[512,1024]{1,0:T(8,128)}) fusion(), kind=kLoop, calls=%fused_computation.14 | loop fusion | flops 7864320 | bytes 4194304 | tf_op jit(solution)/shard_map/neg | solution.py:19
  15.7 1.1 reshape.198
  16.9 4.6 %fusion.13 = bf16[1024,8,128]{2,0,1:T(8,128)(2,1)S(1)} fusion(bf16[8,1024,128]{2,1,0:T(8,128)(2,1)S(1)} %copy-done, f32[512,1024]{1,0:T(8,128)} %get-tuple-element.22, f32[512,1024]{1,0:T(8,128)} %get-tuple-element.23), kind=kOutput, calls=%fused_computation.18 | convolution fusion | flops 2151677952 | bytes 8388608 | tf_op jit(solution)/shard_map/kt,xts->xks/dot_general | solution.py:82
  23.8 37.8 %all-reduce.3.cloned.1.call-done = f32[4,2,64,128]{3,2,0,1:T(8,128)} async-done(((f32[4,2,64,128]{3,2,0,1:T(8,128)}), f32[4,2,64,128]{3,2,0,1:T(8,128)}) %all-reduce.3.cloned.1.call-update) | async-done | bytes 262160
  61.6 2.1 %dynamic-slice_bitcast_fusion = f32[2,64,128]{2,1,0:T(8,128)} fusion(f32[4,2,64,128]{3,2,0,1:T(8,128)} %all-reduce.3.cloned.1.call-done, u32[]{:T(128)} %bitcast.63), kind=kLoop, calls=%fused_computation.55 | loop fusion | bytes 131076 | tf_op jit(solution)/shard_map/squeeze | solution.py:98
  64.3 6.9 %reduce-scatter.5.cloned.1.call-done = f32[2,32,128]{2,1,0:T(8,128)} async-done(((f32[2,64,128]{2,1,0:T(8,128)}), f32[2,32,128]{2,1,0:T(8,128)}) %reduce-scatter.5.cloned.1.call-update) | async-done | bytes 32784 | tf_op jit(solution)/shard_map/reduce_scatter | solution.py:99
  71.3 1.7 %collective-permute-start = (f32[2,32,128]{2,1,0:T(8,128)}, f32[2,32,128]{2,1,0:T(8,128)S(1)}, u32[]{:S(2)}, u32[]{:S(2)}) collective-permute-start(f32[2,32,128]{2,1,0:T(8,128)} %reduce-scatter.5.cloned.1.call-done), channel_id=1, source_target_pairs={{0,2},{2,0},{1,3},{3,1},{4,6},{6,4},{5,7},{7,5},{8,10},{10,8},{9,1... | collective-permute-start | bytes 98312 | tf_op jit(solution)/shard_map/ppermute | solution.py:10
  78.2 1.8 %all_gather.18 = f32[2,64,128]{2,1,0:T(8,128)S(1)} all-gather(f32[2,32,128]{2,1,0:T(8,128)S(1)} %get-tuple-element.10), channel_id=1, replica_groups=mesh['groups'=2,'trace'=4,'space'=2,'sub'=2] {'sub'}, dimensions={1}, use_global_device_ids=true | all-gather | bytes 98304 | tf_op jit(solution)/shard_map/all_gather | solution.py:54
  80.9 0.9 fusion.38
  81.8 1.9 %all_gather.19 = f32[2,64,128]{2,1,0:T(8,128)S(1)} all-gather(f32[2,32,128]{2,1,0:T(8,128)S(1)} %get-tuple-element.9), channel_id=1, replica_groups=mesh['groups'=2,'trace'=4,'space'=2,'sub'=2] {'sub'}, dimensions={1}, use_global_device_ids=true | all-gather | bytes 98304 | tf_op jit(solution)/shard_map/all_gather | solution.py:55
  84.5 0.9 fusion.40
  85.4 0.9 fusion.29
  86.3 0.9 fusion.30
  87.1 0.9 fusion.27
  88.0 0.9 fusion.28
  88.9 1.6 %collective-permute-start.1 = (f32[2,32,128]{2,1,0:T(8,128)S(1)}, f32[2,32,128]{2,1,0:T(8,128)S(1)}, u32[]{:S(2)}, u32[]{:S(2)}) collective-permute-start(f32[2,32,128]{2,1,0:T(8,128)S(1)} %maximum_add_fusion), channel_id=1, source_target_pairs={{0,4},{4,0},{8,12},{12,8},{1,5},{5,1},{9,13},{13,9},{2,6},{6,2},{1... | collective-permute-start | bytes 98312 | tf_op jit(solution)/shard_map/ppermute | solution.py:10
  94.4 1.9 %all_gather.20 = f32[2,64,128]{2,1,0:T(8,128)S(1)} all-gather(f32[2,32,128]{2,1,0:T(8,128)S(1)} %get-tuple-element.8), channel_id=1, replica_groups=mesh['groups'=2,'trace'=4,'space'=2,'sub'=2] {'sub'}, dimensions={1}, use_global_device_ids=true | all-gather | bytes 98304 | tf_op jit(solution)/shard_map/all_gather | solution.py:54
  97.1 0.9 fusion.42
  98.0 1.9 %all_gather.21 = f32[2,64,128]{2,1,0:T(8,128)S(1)} all-gather(f32[2,32,128]{2,1,0:T(8,128)S(1)} %get-tuple-element.7), channel_id=1, replica_groups=mesh['groups'=2,'trace'=4,'space'=2,'sub'=2] {'sub'}, dimensions={1}, use_global_device_ids=true | all-gather | bytes 98304 | tf_op jit(solution)/shard_map/all_gather | solution.py:55
  100.7 0.9 fusion.44
  101.6 0.9 fusion.25
  102.5 0.9 fusion.26
  103.3 0.9 fusion.23
  104.2 0.9 fusion.24
  105.1 2.5 %collective-permute-start.2 = (f32[2,32,128]{2,1,0:T(8,128)S(1)}, f32[2,32,128]{2,1,0:T(8,128)S(1)}, u32[]{:S(2)}, u32[]{:S(2)}) collective-permute-start(f32[2,32,128]{2,1,0:T(8,128)S(1)} %maximum_add_fusion.1), channel_id=1, source_target_pairs={{0,8},{4,12},{8,0},{12,4},{1,9},{5,13},{9,1},{13,5},{2,10},{6,14},... | collective-permute-start | bytes 98312 | tf_op jit(solution)/shard_map/ppermute | solution.py:10
  112.2 1.9 %all_gather.22 = f32[2,64,128]{2,1,0:T(8,128)S(1)} all-gather(f32[2,32,128]{2,1,0:T(8,128)S(1)} %get-tuple-element.6), channel_id=1, replica_groups=mesh['groups'=2,'trace'=4,'space'=2,'sub'=2] {'sub'}, dimensions={1}, use_global_device_ids=true | all-gather | bytes 98304 | tf_op jit(solution)/shard_map/all_gather | solution.py:54
  115.0 0.9 fusion.46
  115.8 1.9 %all_gather.23 = f32[2,64,128]{2,1,0:T(8,128)S(1)} all-gather(f32[2,32,128]{2,1,0:T(8,128)S(1)} %get-tuple-element.5), channel_id=1, replica_groups=mesh['groups'=2,'trace'=4,'space'=2,'sub'=2] {'sub'}, dimensions={1}, use_global_device_ids=true | all-gather | bytes 98304 | tf_op jit(solution)/shard_map/all_gather | solution.py:55
  118.6 0.9 fusion.48
  119.5 0.9 fusion.21
  120.3 0.9 fusion.22
  121.2 0.9 fusion.19
  (47 shorter events, 11.6 us)
Async XLA Ops:
  6.5 10.3 %copy-start = (bf16[8,1024,128]{2,1,0:T(8,128)(2,1)S(1)}, bf16[8,1024,128]{2,1,0:T(8,128)(2,1)}, u32[]{:S(2)}) copy-start(bf16[8,1024,128]{2,1,0:T(8,128)(2,1)} %param.6) | copy-start | bytes 6291460
  6.5 9.2 %copy-start.1 = (bf16[8,512,2,64]{1,3,2,0:T(8,128)(2,1)S(1)}, bf16[8,512,2,64]{1,3,2,0:T(8,128)(2,1)}, u32[]{:S(2)}) copy-start(bf16[8,512,2,64]{1,3,2,0:T(8,128)(2,1)} %param.9) | copy-start | bytes 3145732
  6.5 55.1 %all-reduce.3.cloned.1.call-start = ((), (), s32[]{:S(2)}) async-start(), calls=%async_computation.2 | async-start | bytes 524288
  16.9 4.7 %copy-start.4 = (s32[128]{0:T(128)S(1)}, s32[128]{0:T(128)}, u32[]{:S(2)}) copy-start(s32[128]{0:T(128)} %param.8) | copy-start | bytes 1540
  16.9 4.7 %copy-start.5 = (s32[128]{0:T(128)S(1)}, s32[128]{0:T(128)}, u32[]{:S(2)}) copy-start(s32[128]{0:T(128)} %param.7) | copy-start | bytes 1540
  16.9 4.8 %copy-start.2 = (bf16[8,4,128,2,64]{2,1,4,3,0:T(4,128)(2,1)S(1)}, bf16[8,4,128,2,64]{2,1,4,3,0:T(4,128)(2,1)}, u32[]{:S(2)}) copy-start(bf16[8,4,128,2,64]{2,1,4,3,0:T(4,128)(2,1)} %reshape.198) | copy-start | bytes 3145732
  21.7 1.5 %copy-start.6 = (u32[32]{0:T(128)S(1)}, u32[32]{0:T(128)}, u32[]{:S(2)}) copy-start(u32[32]{0:T(128)} %constant.238) | copy-start | bytes 388
  21.7 2.1 %copy-start.3 = (s32[3,8,2]{1,2,0:T(2,128)S(1)}, s32[3,8,2]{1,2,0:T(2,128)}, u32[]{:S(2)}) copy-start(s32[3,8,2]{1,2,0:T(2,128)} %param.11) | copy-start | bytes 580
  23.1 48.2 %reduce-scatter.5.cloned.1.call-start = ((), (), s32[]{:S(2)}) async-start(), calls=%async_computation.1 | async-start | bytes 98304 | tf_op jit(solution)/shard_map/reduce_scatter | solution.py:99
  71.3 6.1 %collective-permute-start = (f32[2,32,128]{2,1,0:T(8,128)}, f32[2,32,128]{2,1,0:T(8,128)S(1)}, u32[]{:S(2)}, u32[]{:S(2)}) collective-permute-start(f32[2,32,128]{2,1,0:T(8,128)} %reduce-scatter.5.cloned.1.call-done), channel_id=1, source_target_pairs={{0,2},{2,0},{1,3},{3,1},{4,6},{6,4},{5,7},{7,5},{8,10},{10,8},{9,1... | collective-permute-start | bytes 98312 | tf_op jit(solution)/shard_map/ppermute | solution.py:10
  88.9 5.4 %collective-permute-start.1 = (f32[2,32,128]{2,1,0:T(8,128)S(1)}, f32[2,32,128]{2,1,0:T(8,128)S(1)}, u32[]{:S(2)}, u32[]{:S(2)}) collective-permute-start(f32[2,32,128]{2,1,0:T(8,128)S(1)} %maximum_add_fusion), channel_id=1, source_target_pairs={{0,4},{4,0},{8,12},{12,8},{1,5},{5,1},{9,13},{13,9},{2,6},{6,2},{1... | collective-permute-start | bytes 98312 | tf_op jit(solution)/shard_map/ppermute | solution.py:10
  105.1 7.1 %collective-permute-start.2 = (f32[2,32,128]{2,1,0:T(8,128)S(1)}, f32[2,32,128]{2,1,0:T(8,128)S(1)}, u32[]{:S(2)}, u32[]{:S(2)}) collective-permute-start(f32[2,32,128]{2,1,0:T(8,128)S(1)} %maximum_add_fusion.1), channel_id=1, source_target_pairs={{0,8},{4,12},{8,0},{12,4},{1,9},{5,13},{9,1},{13,5},{2,10},{6,14},... | collective-permute-start | bytes 98312 | tf_op jit(solution)/shard_map/ppermute | solution.py:10
Sparse Core Ops, SparseCore 0:
  23.2 38.3 all-reduce.2
  63.9 7.3 reduce-scatter.4
where the time goes:
time: 133 us; the launch traced here: 130 us
  waiting for transfers between devices  44.8 us (34%)
  matrix products  26.3 us (20%)
  between operations  25.3 us (19%)
  other arithmetic  11.5 us (9%)
  blocking collectives  11.1 us (8%)
  starting transfers between devices  5.76 us (4%)
  local copies, waits for them, and re-layouts  5.69 us (4%)
    unnamed x3, waiting for transfers between devices  37.9 us
    neg x1, other arithmetic, spectral_table(): -jnp.sin(angle)  9.19 us
    reduce_scatter x1, waiting for transfers between devices, per_device(): lax.psum_scatter(leaf_terms, 'sub', scatter_dimension=1, tiled=True)  6.95 us
    ppermute x3, starting transfers between devices, swapped(): lax.ppermute(x, axis, [(i, i ^ 1 << distance) for i in range(lax.axis_siz...  5.71 us
    all_gather x3, blocking collectives, merge_level(): lax.all_gather(upper_part, 'sub', axis=1, tiled=True)  5.57 us
    all_gather x3, blocking collectives, merge_level(): lax.all_gather(lower_part, 'sub', axis=1, tiled=True)  5.55 us
    dot_general x6, matrix products, complex_product(): jnp.dot(left[1], right[1], precision=highest)  5.28 us
    dot_general x6, matrix products, complex_product(): jnp.dot(left[0], right[1], precision=highest)  5.28 us
  transfers between devices with their start and end apart: 5, of which 2 were waited for; matrix products, arithmetic and copies ran while one was open for 2% of the time, Pallas kernels for 0%

commit v1 on v0

v1 whole, which is shorter than its diff:
```python
import functools
import math

import jax
import jax.numpy as jnp
import numpy as np
from jax import lax
from jax.experimental import pallas as pl
from jax.experimental.pallas import tpu as pltpu
from jax.sharding import PartitionSpec as P

CHUNK = 128


def spectral_rows(freq_total, samples, chunk):
    phase = (np.arange(freq_total)[:, None] * np.arange(samples)[None, :]) % samples
    angle = phase.astype(np.float32) * np.float32(2.0 * math.pi / samples)
    factor = np.float32(1.0 / math.sqrt(samples))
    rows = np.stack([np.cos(angle) * factor, -np.sin(angle) * factor])
    rows = rows.reshape(2, freq_total // chunk, chunk, samples).swapaxes(0, 1)
    return rows.reshape(freq_total // chunk, 2 * chunk, samples).astype(jnp.bfloat16)


def halves(x):
    high = x.astype(jnp.bfloat16)
    return high, (x - high.astype(jnp.float32)).astype(jnp.bfloat16)


def reversed_bits(index, bits):
    out = 0
    for bit in range(bits):
        out = out | (((index >> bit) & 1) << (bits - 1 - bit))
    return out


def source_kernel(
    sizes,
    place_ref,
    table_ref,
    low_ref,
    high_ref,
    seismic_hbm,
    rows_hbm,
    leaf_hbm,
    moves_hbm,
    keep_ref,
    send_ref,
    seismic_ref,
    rows_ref,
    leaf_ref,
    moves_ref,
    spectra_ref,
    now_ref,
    next_ref,
    sems,
):
    traces, samples, shots, freq_total, rank, bands, spaces, subs = sizes
    chunks = freq_total // CHUNK
    freq_block = freq_total // bands
    boxes = bands * spaces
    box_bits = boxes.bit_length() - 1
    sub_bits = subs.bit_length() - 1
    space_bits = spaces.bit_length() - 1
    part = rank // subs
    own_box, own_space, own_sub = place_ref[0], place_ref[1], place_ref[2]

    copies = []
    for source, target in (
        [(rows_hbm.at[0], rows_ref.at[0])]
        + [(seismic_hbm.at[j], seismic_ref.at[j]) for j in range(traces)]
        + [(leaf_hbm, leaf_ref)]
        + [(rows_hbm.at[c], rows_ref.at[c]) for c in range(1, chunks)]
        + [(moves_hbm, moves_ref)]
    ):
        copy = pltpu.make_async_copy(source, target, sems.at[len(copies)])
        copy.start()
        copies.append(copy)
    copies[0].wait()

    for c in range(chunks):
        if c > 0:
            copies[traces + 1 + c].wait()
        freq = lax.broadcasted_iota(jnp.int32, (CHUNK, shots), 0) + c * CHUNK
        kept = (freq >= low_ref[...]) & (freq < high_ref[...])
        for j in range(0, traces, 2):
            if c == 0:
                copies[1 + j].wait()
                copies[2 + j].wait()
            pair = jnp.concatenate([seismic_ref[j], seismic_ref[j + 1]], axis=1)
            spectra = jnp.dot(rows_ref[c], pair, preferred_element_type=jnp.float32)
            for k in range(2):
                cut = spectra[:, k * shots : (k + 1) * shots]
                for part_no in range(2):
                    piece = cut[part_no * CHUNK : (part_no + 1) * CHUNK]
                    piece = jnp.where(kept, piece, 0.0).astype(jnp.bfloat16)
                    spectra_ref[c, pl.ds((j + k) * CHUNK, CHUNK), pl.ds(part_no * shots, shots)] = piece
    copies[traces + 1].wait()
    copies[traces + 1 + chunks].wait()
    for g in range(bands):
        first = g * freq_block
        total = None
        for start in range(first, first + freq_block, min(freq_block, CHUNK)):
            c, offset = start // CHUNK, start % CHUNK
            width = min(freq_block, CHUNK)
            for j in range(traces):
                term = jnp.dot(
                    leaf_ref[j, :, pl.ds(start, width)],
                    spectra_ref[c, pl.ds(j * CHUNK + offset, width), :],
                    preferred_element_type=jnp.float32,
                )
                total = term if total is None else total + term
        now_ref[g, :rank] = total[:rank, :shots] - total[rank:, shots:]
        now_ref[g, rank:] = total[rank:, :shots] + total[:rank, shots:]

    def complex_rows(entry):
        real, imag = moves_ref[entry, 0], moves_ref[entry, 1]
        return jnp.concatenate(
            [jnp.concatenate([real, -imag], axis=1), jnp.concatenate([imag, real], axis=1)], axis=0
        )

    def level(section_no, source, store):
        stride = 1 << section_no
        inside = section_no < space_bits
        count = boxes // 2 if not inside else bands * (1 << section_no)

        def body(i, carry):
            if inside:
                done = i % stride
                band = i // stride
                above = (own_space >> (section_no + 1)) << (section_no + 1)
                lower = band * spaces + above + done
                own_bit = (own_space >> section_no) & 1
                right = source[i]
                mats = [
                    complex_rows(table_ref[(section_no * boxes + lower + upper * stride) * 2 + own_bit])
                    for upper in range(2)
                ]
                places = [band * (2 * stride) + upper * stride + done for upper in range(2)]
            else:
                lower = (i // stride) * (2 * stride) + i % stride
                right = jnp.concatenate([source[lower], source[lower + stride]], axis=0)
                mats = [
                    jnp.concatenate(
                        [
                            complex_rows(table_ref[(section_no * boxes + lower + upper * stride) * 2 + child])
                            for child in range(2)
                        ],
                        axis=1,
                    )
                    for upper in range(2)
                ]
                places = [lower, lower + stride]
            left_high, left_low = halves(jnp.concatenate(mats, axis=0))
            right_high, right_low = halves(right)
            left = jnp.concatenate([left_high, left_low], axis=0)
            wide = jnp.concatenate([right_high, right_low], axis=1)
            product = jnp.dot(left, wide, preferred_element_type=jnp.float32)
            product = product[:, :shots] + product[:, shots:]
            product = product[: 4 * rank] + product[4 * rank :]
            for upper in range(2):
                store(places[upper], product[upper * 2 * rank : (upper + 1) * 2 * rank])
            return carry

        lax.fori_loop(0, count, body, 0, unroll=count <= 4)

    def store_last(box, value):
        place = reversed_bits(box ^ own_box, box_bits)
        for half in range(subs):
            across = reversed_bits(half ^ own_sub, sub_bits)
            rows = jnp.stack([value[half * part : (half + 1) * part], value[rank + half * part : rank + (half + 1) * part]])

            @pl.when(across < subs // 2)
            def _():
                keep_ref[across * boxes + place] = rows

            @pl.when(across >= subs // 2)
            def _():
                send_ref[(across - subs // 2) * boxes + place] = rows.astype(jnp.bfloat16)

    def store_in(ref):
        def store(box, value):
            ref[box] = value

        return store

    sources = [now_ref, next_ref]
    for section_no in range(box_bits):
        last = section_no == box_bits - 1
        level(section_no, sources[section_no % 2], store_last if last else store_in(sources[(section_no + 1) % 2]))


def per_device(seismic, band_low, band_high, leaf_weights, translations, level_table):
    bands, spaces, subs = (lax.axis_size(name) for name in ("trace", "space", "sub"))
    traces, samples, shots = seismic.shape
    freq_total, rank = leaf_weights.shape[1], leaf_weights.shape[3]
    boxes = bands * spaces
    chunks = freq_total // CHUNK
    own_space = lax.axis_index("space")
    own_box = lax.axis_index("trace") * spaces + own_space
    place = jnp.stack([own_box, own_space, lax.axis_index("sub")]).astype(jnp.int32)
    rows = jnp.asarray(spectral_rows(freq_total, samples, CHUNK))
    leaf = leaf_weights.transpose(0, 2, 3, 1).reshape(traces, 2 * rank, freq_total)
    out_rows = subs // 2 * boxes
    tail = (2, rank // subs, shots)
    smem = pl.BlockSpec(memory_space=pltpu.SMEM)
    vmem = pl.BlockSpec(memory_space=pltpu.VMEM)
    anywhere = pl.BlockSpec(memory_space=pl.ANY)
    keep, send = pl.pallas_call(
        functools.partial(source_kernel, (traces, samples, shots, freq_total, rank, bands, spaces, subs)),
        out_shape=(
            jax.ShapeDtypeStruct((out_rows,) + tail, jnp.float32),
            jax.ShapeDtypeStruct((out_rows,) + tail, jnp.bfloat16),
        ),
        in_specs=[smem, smem, vmem, vmem] + [anywhere] * 4,
        out_specs=(vmem, vmem),
        scratch_shapes=[
            pltpu.VMEM(seismic.shape, jnp.bfloat16),
            pltpu.VMEM(rows.shape, jnp.bfloat16),
            pltpu.VMEM(leaf.shape, jnp.bfloat16),
            pltpu.VMEM(translations.shape, jnp.float32),
            pltpu.VMEM((chunks, traces * CHUNK, 2 * shots), jnp.bfloat16),
            pltpu.VMEM((boxes, 2 * rank, shots), jnp.float32),
            pltpu.VMEM((boxes, 2 * rank, shots), jnp.float32),
            pltpu.SemaphoreType.DMA((traces + chunks + 2,)),
        ],
        name="source",
    )(
        place,
        level_table.reshape(-1),
        band_low[None, :],
        band_high[None, :],
        seismic,
        rows,
        leaf,
        translations,
    )

    def swapped(x, axis, bit):
        return lax.ppermute(x, axis, [(i, i ^ 1 << bit) for i in range(lax.axis_size(axis))])

    steps = [(axis, bit) for axis in ("sub", "space", "trace") for bit in range(lax.axis_size(axis).bit_length() - 1)]
    for axis, bit in steps:
        total = keep + swapped(send, axis, bit).astype(jnp.float32)
        half = total.shape[0] // 2
        keep, send = total[:half], total[half:].astype(jnp.bfloat16)
    return total


def solution(mesh):
    placed = (
        P(("groups", "trace", "space", "sub"), None, None),
        P("groups"),
        P("groups"),
        P(),
        P(),
        P(),
    )
    return jax.shard_map(
        per_device,
        mesh=mesh,
        in_specs=placed,
        out_specs=P(("groups", "trace", "space"), None, "sub", None),
        check_vma=False,
    )
```

time: 133 us -> 28.9 us (0.22); the launches traced: 130 us -> 28.7 us
  waiting for transfers between devices: 44.8 us -> 7.29 us
  matrix products: 26.3 us -> 0 us
  between operations: 25.3 us -> 0.05 us
  blocking collectives: 11.1 us -> 0 us
  other arithmetic: 11.5 us -> 2.23 us
  Pallas kernels: 0 us -> 9.12 us
  local copies, waits for them, and re-layouts: 5.69 us -> 1.48 us
  starting transfers between devices: 5.76 us -> 8.49 us
    unnamed x3 -> x0, waiting for transfers between devices: 37.9 us -> none
    dot_general x26 -> x0, matrix products: 26.3 us -> none  [the longest x6 5.28 us: complex_product(): jnp.dot(left[1], right[1], precision=highest)]
    all_gather x6 -> x0, blocking collectives: 11.1 us -> none  [the longest x3 5.57 us: merge_level(): lax.all_gather(upper_part, 'sub', axis=1, tiled=True)]
    neg x1 -> x0, other arithmetic: 9.19 us -> none  [spectral_table(): -jnp.sin(angle)]
    pallas_call x0 -> x1, Pallas kernels: none -> 9.12 us  [per_device(): pl.pallas_call(functools.partial(source_kernel, (traces, samples, shots,...]
    ppermute x3 -> x4, waiting for transfers between devices: 0.01 us -> 7.29 us  [swapped(): lax.ppermute(x, axis, [(i, i ^ 1 << bit) for i in range(lax.axis_size(axi...]
    reduce_scatter x1 -> x0, waiting for transfers between devices: 6.95 us -> none  [per_device(): lax.psum_scatter(leaf_terms, 'sub', scatter_dimension=1, tiled=True)]
    ppermute x3 -> x4, starting transfers between devices: 5.71 us -> 8.49 us  [swapped(): lax.ppermute(x, axis, [(i, i ^ 1 << bit) for i in range(lax.axis_size(axi...]
  transfers between devices with their start and end apart: 5 -> 4, of which waited for: 2 -> 4; matrix products, arithmetic and copies ran while one was open for 2% -> 0% of each run, Pallas kernels for 0% -> 0%
where the time goes in v1:
time: 28.9 us; the launch traced here: 28.7 us
  Pallas kernels  9.12 us (32%)
  starting transfers between devices  8.49 us (29%)
  waiting for transfers between devices  7.29 us (25%)
  other arithmetic  2.23 us (8%)
  local copies, waits for them, and re-layouts  1.48 us (5%)
    pallas_call x1, Pallas kernels, per_device(): pl.pallas_call(functools.partial(source_kernel, (traces, samples, shots,...  9.12 us
    ppermute x4, starting transfers between devices, swapped(): lax.ppermute(x, axis, [(i, i ^ 1 << bit) for i in range(lax.axis_size(axi...  8.49 us
    ppermute x4, waiting for transfers between devices, swapped(): lax.ppermute(x, axis, [(i, i ^ 1 << bit) for i in range(lax.axis_size(axi...  7.29 us
    add x4, other arithmetic, per_device(): total = keep + swapped(send, axis, bit).astype(jnp.float32)  1.63 us
    unnamed x1, local copies, waits for them, and re-layouts  0.77 us
    reshape x1, local copies, waits for them, and re-layouts, per_device(): level_table.reshape(-1)  0.69 us
    another operation x1, other arithmetic, per_device(): jnp.stack([own_box, own_space, lax.axis_index('sub')]).astype(jnp.int32)  0.61 us
  transfers between devices with their start and end apart: 4, of which 4 were waited for; matrix products, arithmetic and copies ran while one was open for 0% of the time, Pallas kernels for 0%

profile of v1, /device:TPU:0, one launch (start us, length us, event | category | flops | bytes accessed | tf_op | source)
XLA Modules:
  0.0 28.7 jit_solution(13217073691371399578)
XLA Ops:
  0.0 0.8 %copy.9 = s32[3,8,2]{2,1,0:T(8,128)S(1)} copy(s32[3,8,2]{1,2,0:T(2,128)} %param.12) | data formatting | bytes 384 | tf_op args[5]
  0.8 0.7 %reshape.6.table_ref = s32[48]{0:T(128)} reshape(s32[3,8,2]{2,1,0:T(8,128)S(1)} %copy.9) | data formatting | bytes 384 | tf_op jit(solution)/shard_map/reshape | solution.py:229
  1.5 0.6 %pad_add_fusion.place_ref = s32[3]{0:T(128)} fusion(s32[1]{0:T(128)} %bitcast.2, s32[1]{0:T(128)} %bitcast.1, s32[1]{0:T(128)} %bitcast), kind=kLoop, calls=%fused_computation.7 | loop fusion | flops 6 | bytes 24 | tf_op jit(solution)/shard_map/stack | solution.py:200
  2.1 9.1 %source.1 = (f32[8,2,32,128]{3,2,1,0:T(8,128)}, bf16[8,2,32,128]{3,2,1,0:T(8,128)(2,1)}) custom-call(s32[3]{0:T(128)} %pad_add_fusion.place_ref, s32[48]{0:T(128)} %reshape.6.table_ref, s32[1,128]{1,0:T(1,128)} %bitcast.9, s32[1,128]{1,0:T(1,128)} %bitcast.10, bf16[8,1024,128]{2,1,0:T(8,128)(2,1)} %seismic_hbm.1, ...), custom_call_target="tpu_custom_call" | custom-call | tf_op jit(solution)/shard_map/source/pallas_call | solution.py:208
  11.2 0.5 %collective-permute-start = (bf16[8,2,32,128]{3,2,1,0:T(8,128)(2,1)}, bf16[8,2,32,128]{3,2,1,0:T(8,128)(2,1)S(1)}, u32[]{:S(2)}, u32[]{:S(2)}) collective-permute-start(bf16[8,2,32,128]{3,2,1,0:T(8,128)(2,1)} %get-tuple-element.8), channel_id=1, source_target_pairs={{0,1},{1,0},{2,3},{3,2},{4,5},{5,4},{6,7},{7,6},{8,9},{9,8},{10,11... | collective-permute-start | bytes 393224 | tf_op jit(solution)/shard_map/ppermute | solution.py:239
  11.8 1.2 %collective-permute-done = bf16[8,2,32,128]{3,2,1,0:T(8,128)(2,1)S(1)} collective-permute-done((bf16[8,2,32,128]{3,2,1,0:T(8,128)(2,1)}, bf16[8,2,32,128]{3,2,1,0:T(8,128)(2,1)S(1)}, u32[]{:S(2)}, u32[]{:S(2)}) %collective-permute-start) | collective-permute-done | bytes 131104 | tf_op jit(solution)/shard_map/ppermute | solution.py:239
  12.9 1.0 %convert_add_fusion = f32[8,2,32,128]{3,2,1,0:T(8,128)S(1)} fusion(f32[8,2,32,128]{3,2,1,0:T(8,128)} %get-tuple-element.7, bf16[8,2,32,128]{3,2,1,0:T(8,128)(2,1)S(1)} %collective-permute-done), kind=kLoop, calls=%fused_computation | loop fusion | flops 131072 | bytes 655360 | tf_op jit(solution)/shard_map/add | solution.py:243
  14.0 2.9 %collective-permute-start.1 = (bf16[4,2,32,128]{3,2,1,0:T(8,128)(2,1)S(1)}, bf16[4,2,32,128]{3,2,1,0:T(8,128)(2,1)S(1)}, u32[]{:S(2)}, u32[]{:S(2)}) collective-permute-start(bf16[4,2,32,128]{3,2,1,0:T(8,128)(2,1)S(1)} %slice.39), channel_id=1, source_target_pairs={{0,2},{2,0},{1,3},{3,1},{4,6},{6,4},{5,7},{7,5},{8,10},{10,8},{9,1... | collective-permute-start | bytes 196616 | tf_op jit(solution)/shard_map/ppermute | solution.py:239
  16.9 2.4 %collective-permute-done.1 = bf16[4,2,32,128]{3,2,1,0:T(8,128)(2,1)S(1)} collective-permute-done((bf16[4,2,32,128]{3,2,1,0:T(8,128)(2,1)S(1)}, bf16[4,2,32,128]{3,2,1,0:T(8,128)(2,1)S(1)}, u32[]{:S(2)}, u32[]{:S(2)}) %collective-permute-start.1) | collective-permute-done | bytes 65568 | tf_op jit(solution)/shard_map/ppermute | solution.py:239
  19.3 2.0 %collective-permute-start.2 = (bf16[2,2,32,128]{3,2,1,0:T(8,128)(2,1)S(1)}, bf16[2,2,32,128]{3,2,1,0:T(8,128)(2,1)S(1)}, u32[]{:S(2)}, u32[]{:S(2)}) collective-permute-start(bf16[2,2,32,128]{3,2,1,0:T(8,128)(2,1)S(1)} %slice.40), channel_id=1, source_target_pairs={{0,4},{4,0},{8,12},{12,8},{1,5},{5,1},{9,13},{13,9},{2,6},{6,2},{1... | collective-permute-start | bytes 98312 | tf_op jit(solution)/shard_map/ppermute | solution.py:239
  21.3 2.0 %collective-permute-done.2 = bf16[2,2,32,128]{3,2,1,0:T(8,128)(2,1)S(1)} collective-permute-done((bf16[2,2,32,128]{3,2,1,0:T(8,128)(2,1)S(1)}, bf16[2,2,32,128]{3,2,1,0:T(8,128)(2,1)S(1)}, u32[]{:S(2)}, u32[]{:S(2)}) %collective-permute-start.2) | collective-permute-done | bytes 32800 | tf_op jit(solution)/shard_map/ppermute | solution.py:239
  23.3 3.0 %collective-permute-start.3 = (bf16[1,2,32,128]{3,2,1,0:T(8,128)(2,1)S(1)}, bf16[1,2,32,128]{3,2,1,0:T(8,128)(2,1)S(1)}, u32[]{:S(2)}, u32[]{:S(2)}) collective-permute-start(bf16[1,2,32,128]{3,2,1,0:T(8,128)(2,1)S(1)} %slice.41), channel_id=1, source_target_pairs={{0,8},{4,12},{8,0},{12,4},{1,9},{5,13},{9,1},{13,5},{2,10},{6,14},... | collective-permute-start | bytes 49160 | tf_op jit(solution)/shard_map/ppermute | solution.py:239
  26.3 1.7 %collective-permute-done.3 = bf16[1,2,32,128]{3,2,1,0:T(8,128)(2,1)S(1)} collective-permute-done((bf16[1,2,32,128]{3,2,1,0:T(8,128)(2,1)S(1)}, bf16[1,2,32,128]{3,2,1,0:T(8,128)(2,1)S(1)}, u32[]{:S(2)}, u32[]{:S(2)}) %collective-permute-start.3) | collective-permute-done | bytes 16416 | tf_op jit(solution)/shard_map/ppermute | solution.py:239
  28.1 0.6 %slice_add_fusion.2 = f32[1,2,32,128]{3,2,1,0:T(8,128)} fusion(f32[2,2,32,128]{3,2,1,0:T(8,128)S(1)} %slice_add_fusion.1, bf16[1,2,32,128]{3,2,1,0:T(8,128)(2,1)S(1)} %collective-permute-done.3), kind=kLoop, calls=%fused_computation.6 | loop fusion | flops 16384 | bytes 81920 | tf_op jit(solution)/shard_map/add | solution.py:243
  (5 shorter events, 0.0 us)
Async XLA Ops:
  11.2 1.7 %collective-permute-start = (bf16[8,2,32,128]{3,2,1,0:T(8,128)(2,1)}, bf16[8,2,32,128]{3,2,1,0:T(8,128)(2,1)S(1)}, u32[]{:S(2)}, u32[]{:S(2)}) collective-permute-start(bf16[8,2,32,128]{3,2,1,0:T(8,128)(2,1)} %get-tuple-element.8), channel_id=1, source_target_pairs={{0,1},{1,0},{2,3},{3,2},{4,5},{5,4},{6,7},{7,6},{8,9},{9,8},{10,11... | collective-permute-start | bytes 393224 | tf_op jit(solution)/shard_map/ppermute | solution.py:239
  14.0 5.3 %collective-permute-start.1 = (bf16[4,2,32,128]{3,2,1,0:T(8,128)(2,1)S(1)}, bf16[4,2,32,128]{3,2,1,0:T(8,128)(2,1)S(1)}, u32[]{:S(2)}, u32[]{:S(2)}) collective-permute-start(bf16[4,2,32,128]{3,2,1,0:T(8,128)(2,1)S(1)} %slice.39), channel_id=1, source_target_pairs={{0,2},{2,0},{1,3},{3,1},{4,6},{6,4},{5,7},{7,5},{8,10},{10,8},{9,1... | collective-permute-start | bytes 196616 | tf_op jit(solution)/shard_map/ppermute | solution.py:239
  19.3 4.0 %collective-permute-start.2 = (bf16[2,2,32,128]{3,2,1,0:T(8,128)(2,1)S(1)}, bf16[2,2,32,128]{3,2,1,0:T(8,128)(2,1)S(1)}, u32[]{:S(2)}, u32[]{:S(2)}) collective-permute-start(bf16[2,2,32,128]{3,2,1,0:T(8,128)(2,1)S(1)} %slice.40), channel_id=1, source_target_pairs={{0,4},{4,0},{8,12},{12,8},{1,5},{5,1},{9,13},{13,9},{2,6},{6,2},{1... | collective-permute-start | bytes 98312 | tf_op jit(solution)/shard_map/ppermute | solution.py:239
  23.3 4.7 %collective-permute-start.3 = (bf16[1,2,32,128]{3,2,1,0:T(8,128)(2,1)S(1)}, bf16[1,2,32,128]{3,2,1,0:T(8,128)(2,1)S(1)}, u32[]{:S(2)}, u32[]{:S(2)}) collective-permute-start(bf16[1,2,32,128]{3,2,1,0:T(8,128)(2,1)S(1)} %slice.41), channel_id=1, source_target_pairs={{0,8},{4,12},{8,0},{12,4},{1,9},{5,13},{9,1},{13,5},{2,10},{6,14},... | collective-permute-start | bytes 49160 | tf_op jit(solution)/shard_map/ppermute | solution.py:239
